TPU v7x, 32 devices: a whole 2x2x4 slice. The times are simulated.
32 devices in a mesh: ia: 4 (over z), ja: 4 (over x, core), aux: 2 (over y).
Axes of the slice: x: 2, y: 2, z: 4, core: 2. Of those that a mesh axis runs over, the one named last changes fastest.
Arguments:
- raw_integrals: bfloat16 [2048, 12, 512], P(('ia', 'ja', 'aux')), may hold values from -0.5 to 0.5
- metric_root: bfloat16 [2048, 2048], replicated, may hold values from -0.125 to 0.125
- eps_occ: float32 [12], replicated, may hold values from -2 to -0.3
- eps_vir: float32 [512], replicated, may hold values from 0.3 to 3
Outputs:
- gamma: float32 [2048, 12, 512], P('ja', 'ia', 'aux')
All inputs are finite; a program needn't handle non-finite values.
Results may differ from a plain program's by a relative error of at most 0.0022.
Values may be sent and summed in bfloat16 or wider, within the bound.
No kernel may reach another device: no remote copies, remote signals or barrier semaphores. Data moves between devices by JAX's collectives and lax.ppermute only.
A program may use at most 128 MiB of HBM per device.

v0:
```python
import jax
import jax.numpy as jnp
from jax import lax
from jax.sharding import PartitionSpec as P

OB = 3
V = 512


def apply_metric(metric_root, raw_rows):
    return lax.dot_general(
        metric_root, raw_rows, (((0,), (0,)), ((), ())), preferred_element_type=jnp.float32
    ).astype(jnp.bfloat16)


def body(raw_integrals, metric_root, eps_occ, eps_vir):
    ia_count = lax.axis_size("ia")
    aux_count = lax.axis_size("aux")
    row_index = lax.axis_index("ia")
    col_index = lax.axis_index("ja")
    aux_index = lax.axis_index("aux")
    pieces = raw_integrals.shape[0]
    aux_total = metric_root.shape[0]
    narrow = V // (ia_count * aux_count)
    half_width = V // aux_count
    by_block = raw_integrals.reshape(pieces, ia_count, OB, ia_count * aux_count, narrow)
    own_rows = by_block.transpose(1, 3, 0, 2, 4).reshape(
        ia_count * ia_count * aux_count, pieces, OB * narrow
    )
    by_column = raw_integrals.reshape(pieces, ia_count, OB, ia_count, aux_count, narrow)
    own_cols = by_column.transpose(3, 1, 4, 0, 2, 5).reshape(
        ia_count * ia_count * aux_count, pieces, OB * narrow
    )
    got_rows, got_cols = (
        lax.all_to_all(own_rows, ("ia", "ja", "aux"), split_axis=0, concat_axis=1, tiled=True),
        lax.all_to_all(own_cols, ("ia", "ja", "aux"), split_axis=0, concat_axis=1, tiled=True),
    )
    joined = jnp.concatenate([got_rows[0], got_cols[0]], axis=1)
    fitted = apply_metric(metric_root, joined)
    row_block = fitted[:, : OB * narrow].reshape(aux_total, OB, narrow)
    col_block = fitted[:, OB * narrow :].reshape(aux_total, OB, narrow)
    block_i = lax.all_gather(row_block, ("ja", "aux"), axis=2, tiled=True)
    block_j = lax.all_gather(col_block, ("ia", "aux"), axis=2, tiled=True)
    half_i = lax.dynamic_slice_in_dim(block_i, aux_index * half_width, half_width, 2)
    half_j = lax.dynamic_slice_in_dim(block_j, aux_index * half_width, half_width, 2)
    flat_i = block_i.reshape(aux_total, OB * V)
    flat_j = block_j.reshape(aux_total, OB * V)
    contract_aux = (((0,), (0,)), ((), ()))
    direct_part = lax.dot_general(
        half_i.reshape(aux_total, OB * half_width),
        flat_j,
        contract_aux,
        preferred_element_type=jnp.float32,
    )
    swap_part = lax.dot_general(
        flat_i,
        half_j.reshape(aux_total, OB * half_width),
        contract_aux,
        preferred_element_type=jnp.float32,
    )
    swap_part = swap_part.reshape(OB, V, OB, half_width).transpose(0, 3, 2, 1)
    energy_i = lax.dynamic_slice_in_dim(eps_occ, row_index * OB, OB, 0)
    energy_j = lax.dynamic_slice_in_dim(eps_occ, col_index * OB, OB, 0)
    energy_a = lax.dynamic_slice_in_dim(eps_vir, aux_index * half_width, half_width, 0)
    denominator = (
        energy_a[None, :, None, None]
        + eps_vir[None, None, None, :]
        - energy_i[:, None, None, None]
        - energy_j[None, None, :, None]
    )
    amplitude = (
        (2.0 * direct_part.reshape(OB, half_width, OB, V) - swap_part) / denominator
    ).astype(jnp.bfloat16)
    amplitude = amplitude.reshape(OB * half_width, OB * V)
    ja_count = lax.axis_size("ja")
    q_rows = aux_total // ja_count
    share = lax.psum_scatter(
        lax.dot_general(
            flat_j, amplitude, (((1,), (1,)), ((), ())), preferred_element_type=jnp.float32
        ),
        "ja",
        scatter_dimension=0,
        tiled=True,
    )
    return share.reshape(q_rows, OB, half_width)


def solution(mesh):
    in_specs = (P(("ia", "ja", "aux"), None, None), P(), P(), P())
    out_specs = P("ja", "ia", "aux")
    return jax.shard_map(body, mesh=mesh, in_specs=in_specs, out_specs=out_specs, check_vma=False)
```

profile of v0, /device:TPU:0, one launch (start us, length us, event | category | flops | bytes accessed | tf_op | source)
XLA Modules:
  0.0 321.8 jit_solution(5210032561810463520)
XLA Ops:
  6.5 3.6 %reshape.91 = bf16[64,4,3,4,2,64]{5,4,3,0,2,1:T(2,128)(2,1)S(1)} reshape(bf16[64,12,512]{2,0,1:T(8,128)(2,1)} %param.4) | data formatting | bytes 1572864 | tf_op jit(solution)/shard_map/reshape | solution.py:30
  10.1 1.8 copy.23
  11.9 1.6 copy.24
  13.5 7.5 %all-to-all-start.1 = ((bf16[32,64,192]{2,1,0:T(8,128)(2,1)}), bf16[32,64,192]{2,1,0:T(8,128)(2,1)}, u32[]{:S(2)}, u32[]{:S(2)}) async-start(bf16[32,64,192]{2,1,0:T(8,128)(2,1)} %copy.24), calls=%async_computation.1 | async-start | bytes 2097152 | tf_op jit(solution)/shard_map/all_to_all | solution.py:36
  20.9 0.0 all-gather.3.cloned.1.call-start
  21.0 2.5 reshape.89
  23.4 1.1 copy.21
  24.6 0.8 copy.22
  25.4 21.8 %all-to-all-done.1 = bf16[32,64,192]{2,1,0:T(8,128)(2,1)} async-done(((bf16[32,64,192]{2,1,0:T(8,128)(2,1)}), bf16[32,64,192]{2,1,0:T(8,128)(2,1)}, u32[]{:S(2)}, u32[]{:S(2)}) %all-to-all-start.1) | async-done | bytes 786464 | tf_op jit(solution)/shard_map/all_to_all | solution.py:36
  47.1 29.6 %all_to_all.8 = bf16[32,64,192]{2,1,0:T(8,128)(2,1)S(1)} all-to-all(bf16[32,64,192]{2,1,0:T(8,128)(2,1)S(1)} %copy.22), channel_id=1, replica_groups=mesh['ia'=4,'ja'=4,'aux'=2] {'ia','ja','aux'}, dimensions={0} | all-to-all | bytes 1572864 | tf_op jit(solution)/shard_map/all_to_all | solution.py:35
  76.7 7.3 %fusion.14 = bf16[2048,384]{0,1:T(8,128)(2,1)S(1)} fusion(bf16[2048,2048]{1,0:T(8,128)(2,1)} %param.5, bf16[2048,192]{1,0:T(8,128)(2,1)} %bitcast.5, bf16[2048,192]{1,0:T(8,128)(2,1)S(1)} %bitcast.80), kind=kOutput, calls=%fused_computation.12 | convolution fusion | flops 3225157632 | bytes 11534336 | tf_op jit(solution)/shard_map/dot_general | solution.py:11
  84.1 0.0 copy-start
  84.1 0.0 copy-start.1
  84.1 1.3 fusion.21
  85.4 0.0 all-gather.3.cloned.1.call-update
  85.4 0.0 all-gather.5.cloned.1.call-start
  85.5 0.7 all-gather.5.cloned.1.call-update
  86.2 0.2 reduce-scatter.2.cloned.1.call-start
  86.4 0.0 copy-done
  86.4 0.1 dynamic_slice.17
  86.5 0.0 copy-done.1
  86.5 0.1 fusion.22
  86.6 0.1 broadcast_add_fusion
  86.7 0.3 broadcast_subtract_fusion
  87.0 96.3 %all-gather.3.cloned.1.call-done = bf16[2048,3,512]{0,2,1:T(8,128)(2,1)} async-done(((bf16[2048,3,64]{0,2,1:T(8,128)(2,1)}), bf16[2048,3,512]{0,2,1:T(8,128)(2,1)}) %all-gather.3.cloned.1.call-update) | async-done | bytes 6291472 | tf_op jit(solution)/shard_map/all_gather | solution.py:43
  183.3 45.5 %all-gather.5.cloned.1.call-done = bf16[2048,3,512]{0,2,1:T(8,128)(2,1)} async-done(((bf16[2048,3,64]{0,2,1:T(8,128)(2,1)}), bf16[2048,3,512]{0,2,1:T(8,128)(2,1)}) %all-gather.5.cloned.1.call-update) | async-done | bytes 6291472 | tf_op jit(solution)/shard_map/all_gather | solution.py:42
  228.8 0.0 copy-start.2
  228.8 0.0 copy-start.3
  228.8 8.4 %fusion = f32[3,512,3,256]{1,3,2,0:T(8,128)S(1)} fusion(bf16[2048,3,512]{0,2,1:T(8,128)(2,1)} %all-gather.5.cloned.1.call-done, bf16[2048,3,512]{0,2,1:T(8,128)(2,1)} %all-gather.3.cloned.1.call-done, s32[]{:T(128)S(6)} %select_n.11), kind=kOutput, calls=%fused_computation | convolution fusion | flops 4831838208 | bytes 14155780 | tf_op jit(solution)/shard_map/dot_general | solution.py:55
  237.2 0.0 copy-done.2
  237.2 0.0 copy-done.3
  237.3 5.6 %fusion.5 = bf16[3,256,3,512]{3,1,2,0:T(8,128)(2,1)S(1)} fusion(f32[3,512,3,256]{1,3,2,0:T(8,128)S(1)} %fusion, bf16[2048,3,512]{0,2,1:T(8,128)(2,1)S(1)} %copy-done.2, bf16[2048,3,512]{0,2,1:T(8,128)(2,1)S(1)} %copy-done.3, s32[]{:T(128)S(6)} %select_n.11, f32[3]{0:T(128)S(1)} %get-tuple-element.8, f32[3,256,512]{2,1,0:T(8,128)S(1)} %broadcast_subtract_fusion), kind=kOutput, calls=%fused_computation.6 | convolution fusion | flops 4837736448 | bytes 18088452 | tf_op jit(solution)/shard_map/dot_general | solution.py:49
  242.9 2.0 copy.26
  244.9 0.8 copy.32
  245.7 7.1 %fusion.23 = f32[2048,768]{1,0:T(8,128)} fusion(bf16[2048,1536]{0,1:T(8,128)(2,1)S(1)} %bitcast.81, bf16[768,1536]{1,0:T(8,128)(2,1)S(1)} %bitcast.79), kind=kOutput, calls=%fused_computation.23 | convolution fusion | flops 4831838208 | bytes 14942208 | tf_op jit(solution)/shard_map/dot_general | solution.py:78
  252.8 0.0 reduce-scatter.2.cloned.1.call-update
  252.8 59.0 %reduce-scatter.2.cloned.1.call-done = f32[512,768]{1,0:T(8,128)} async-done(((f32[2048,768]{1,0:T(8,128)}), f32[512,768]{1,0:T(8,128)}) %reduce-scatter.2.cloned.1.call-update) | async-done | bytes 1572880 | tf_op jit(solution)/shard_map/reduce_scatter | solution.py:77
  311.8 1.9 copy.27
  313.7 1.6 copy.28
Async XLA Ops:
  13.5 33.6 %all-to-all-start.1 = ((bf16[32,64,192]{2,1,0:T(8,128)(2,1)}), bf16[32,64,192]{2,1,0:T(8,128)(2,1)}, u32[]{:S(2)}, u32[]{:S(2)}) async-start(bf16[32,64,192]{2,1,0:T(8,128)(2,1)} %copy.24), calls=%async_computation.1 | async-start | bytes 2097152 | tf_op jit(solution)/shard_map/all_to_all | solution.py:36
  20.9 162.4 %all-gather.3.cloned.1.call-start = ((), (), s32[]{:S(2)}) async-start(), calls=%async_computation.3 | async-start | bytes 7077888 | tf_op jit(solution)/shard_map/all_gather | solution.py:43
  84.1 2.4 copy-start
  84.1 2.4 copy-start.1
  85.4 143.4 %all-gather.5.cloned.1.call-start = ((), (), s32[]{:S(2)}) async-start(), calls=%async_computation.4 | async-start | bytes 7077888 | tf_op jit(solution)/shard_map/all_gather | solution.py:42
  86.2 225.6 %reduce-scatter.2.cloned.1.call-start = ((), (), s32[]{:S(2)}) async-start(), calls=%async_computation.5 | async-start | bytes 7864320 | tf_op jit(solution)/shard_map/reduce_scatter | solution.py:77
  228.8 8.4 %copy-start.2 = (bf16[2048,3,512]{0,2,1:T(8,128)(2,1)S(1)}, bf16[2048,3,512]{0,2,1:T(8,128)(2,1)}, u32[]{:S(2)}) copy-start(bf16[2048,3,512]{0,2,1:T(8,128)(2,1)} %all-gather.3.cloned.1.call-done) | copy-start | bytes 18874372
  228.8 8.4 %copy-start.3 = (bf16[2048,3,512]{0,2,1:T(8,128)(2,1)S(1)}, bf16[2048,3,512]{0,2,1:T(8,128)(2,1)}, u32[]{:S(2)}) copy-start(bf16[2048,3,512]{0,2,1:T(8,128)(2,1)} %all-gather.5.cloned.1.call-done) | copy-start | bytes 18874372
Sparse Core Ops, SparseCore 0:
  85.6 97.7 all-gather.2
  185.2 43.5 all-gather.4
  252.9 58.8 reduce-scatter.1
where the time goes:
time: 322 us
  waiting for transfers between devices  223 us (69%)
  blocking collectives  29.6 us (9%)
  matrix products  28.4 us (9%)
  local copies, waits for them, and re-layouts  19.1 us (6%)
  between operations  13.3 us (4%)
  starting transfers between devices  7.76 us (2%)
    all_gather x1, waiting for transfers between devices, body(): block_j = lax.all_gather(col_block, ('ia', 'aux'), axis=2, tiled=True)  96.3 us
    reduce_scatter x1, waiting for transfers between devices, body(): lax.psum_scatter(lax.dot_general(flat_j, amplitude, (((1,), (1,)), ((), (...  59 us
    all_gather x1, waiting for transfers between devices, body(): block_i = lax.all_gather(row_block, ('ja', 'aux'), axis=2, tiled=True)  45.5 us
    all_to_all x1, blocking collectives, body(): lax.all_to_all(own_rows, ('ia', 'ja', 'aux'), split_axis=0, concat_axis=1...  29.6 us
    all_to_all x1, waiting for transfers between devices, body(): lax.all_to_all(own_cols, ('ia', 'ja', 'aux'), split_axis=0, concat_axis=1...  21.8 us
    dot_general x1, matrix products, body(): lax.dot_general(flat_i, half_j.reshape(aux_total, OB * half_width), contr...  8.42 us
    all_to_all x1, starting transfers between devices, body(): lax.all_to_all(own_cols, ('ia', 'ja', 'aux'), split_axis=0, concat_axis=1...  7.45 us
    dot_general x1, matrix products, apply_metric(): lax.dot_general(metric_root, raw_rows, (((0,), (0,)), ((), ())), preferre...  7.32 us
  transfers between devices with their start and end apart: 4, of which 4 were waited for; matrix products, arithmetic and copies ran while one was open for 2% of the time, Pallas kernels for 0%

commit v1 on v0

--- a/solution.py
+++ b/solution.py
@@ -5,6 +5,27 @@
 
 OB = 3
 V = 512
+
+
+def in_order(pieces, dim):
+    lengths = list(pieces.shape[1:])
+    lengths[dim] *= pieces.shape[0]
+    return jnp.moveaxis(pieces, 0, dim).reshape(lengths)
+
+
+def collected_by_bits(x, axis):
+    size, index = (lax.axis_size(axis), lax.axis_index(axis))
+    tiles, bit = (x[None], 1)
+    while bit < size:
+        received = lax.ppermute(tiles, axis, [(i, i ^ bit) for i in range(size)])
+        low = index & bit == 0
+        tiles = jnp.concatenate([jnp.where(low, tiles, received), jnp.where(low, received, tiles)])
+        bit *= 2
+    return tiles
+
+
+def doubled_up(value, axis, dim):
+    return in_order(collected_by_bits(value, axis), dim)
 
 
 def apply_metric(metric_root, raw_rows):
@@ -39,7 +60,7 @@
     fitted = apply_metric(metric_root, joined)
     row_block = fitted[:, : OB * narrow].reshape(aux_total, OB, narrow)
     col_block = fitted[:, OB * narrow :].reshape(aux_total, OB, narrow)
-    block_i = lax.all_gather(row_block, ("ja", "aux"), axis=2, tiled=True)
+    block_i = doubled_up(row_block, ("ja", "aux"), 2)
     block_j = lax.all_gather(col_block, ("ia", "aux"), axis=2, tiled=True)
     half_i = lax.dynamic_slice_in_dim(block_i, aux_index * half_width, half_width, 2)
     half_j = lax.dynamic_slice_in_dim(block_j, aux_index * half_width, half_width, 2)

time: 322 us -> 291 us (0.904)
  waiting for transfers between devices: 223 us -> 177 us
  other arithmetic: 0.35 us -> 11.1 us
    ppermute x0 -> x3, waiting for transfers between devices: none -> 97.1 us  [collected_by_bits(): received = lax.ppermute(tiles, axis, [(i, i ^ bit) for i in range(size)])]
    all_gather x1, waiting for transfers between devices: 96.3 us -> 0.01 us  [body(): block_j = lax.all_gather(col_block, ('ia', 'aux'), axis=2, tiled=True)]
    all_gather x1 -> x0, waiting for transfers between devices: 45.5 us -> none  [body(): block_i = lax.all_gather(row_block, ('ja', 'aux'), axis=2, tiled=True)]
    concatenate x0 -> x3, other arithmetic: none -> 5.3 us  [collected_by_bits(): jnp.concatenate([jnp.where(low, tiles, received), jnp.where(low, received...]
    select_n x0 -> x3, other arithmetic: none -> 4.28 us  [collected_by_bits(): jnp.where(low, tiles, received)]
    ppermute x0 -> x3, starting transfers between devices: none -> 3.34 us  [collected_by_bits(): received = lax.ppermute(tiles, axis, [(i, i ^ bit) for i in range(size)])]
  transfers between devices with their start and end apart: 4 -> 6, of which waited for: 4 -> 5; matrix products, arithmetic and copies ran while one was open for 2% -> 5% of each run, Pallas kernels for 0% -> 0%
where the time goes in v1:
time: 291 us; the launch traced here: 290 us
  waiting for transfers between devices  177 us (61%)
  blocking collectives  29.6 us (10%)
  matrix products  28.7 us (10%)
  local copies, waits for them, and re-layouts  19.8 us (7%)
  between operations  13.6 us (5%)
  other arithmetic  11.1 us (4%)
  starting transfers between devices  10.9 us (4%)
    ppermute x3, waiting for transfers between devices, collected_by_bits(): received = lax.ppermute(tiles, axis, [(i, i ^ bit) for i in range(size)])  97.1 us
    reduce_scatter x1, waiting for transfers between devices, body(): lax.psum_scatter(lax.dot_general(flat_j, amplitude, (((1,), (1,)), ((), (...  58 us
    all_to_all x1, blocking collectives, body(): lax.all_to_all(own_rows, ('ia', 'ja', 'aux'), split_axis=0, concat_axis=1...  29.6 us
    all_to_all x1, waiting for transfers between devices, body(): lax.all_to_all(own_cols, ('ia', 'ja', 'aux'), split_axis=0, concat_axis=1...  21.8 us
    dot_general x1, matrix products, body(): lax.dot_general(half_i.reshape(aux_total, OB * half_width), flat_j, contr...  8.38 us
    all_to_all x1, starting transfers between devices, body(): lax.all_to_all(own_cols, ('ia', 'ja', 'aux'), split_axis=0, concat_axis=1...  7.45 us
    dot_general x1, matrix products, apply_metric(): lax.dot_general(metric_root, raw_rows, (((0,), (0,)), ((), ())), preferre...  7.32 us
    dot_general x1, matrix products, body(): lax.dot_general(flat_j, amplitude, (((1,), (1,)), ((), ())), preferred_el...  7.07 us
  transfers between devices with their start and end apart: 6, of which 5 were waited for; matrix products, arithmetic and copies ran while one was open for 5% of the time, Pallas kernels for 0%

profile of v1, /device:TPU:0, one launch (start us, length us, event | category | flops | bytes accessed | tf_op | source)
XLA Modules:
  0.0 290.5 jit_solution(9478249513084235052)
XLA Ops:
  6.5 3.6 %reshape.88 = bf16[64,4,3,4,2,64]{5,4,3,0,2,1:T(2,128)(2,1)S(1)} reshape(bf16[64,12,512]{2,0,1:T(8,128)(2,1)} %param.4) | data formatting | bytes 1572864 | tf_op jit(solution)/shard_map/reshape | solution.py:51
  10.1 1.8 copy.29
  11.9 1.6 copy.30
  13.5 7.5 %all-to-all-start.1 = ((bf16[32,64,192]{2,1,0:T(8,128)(2,1)}), bf16[32,64,192]{2,1,0:T(8,128)(2,1)}, u32[]{:S(2)}, u32[]{:S(2)}) async-start(bf16[32,64,192]{2,1,0:T(8,128)(2,1)} %copy.30), calls=%async_computation.1 | async-start | bytes 2097152 | tf_op jit(solution)/shard_map/all_to_all | solution.py:57
  20.9 0.0 all-gather.2.cloned.1.call-start
  21.0 2.5 reshape.86
  23.4 1.1 copy.27
  24.6 0.8 copy.28
  25.4 21.8 %all-to-all-done.1 = bf16[32,64,192]{2,1,0:T(8,128)(2,1)} async-done(((bf16[32,64,192]{2,1,0:T(8,128)(2,1)}), bf16[32,64,192]{2,1,0:T(8,128)(2,1)}, u32[]{:S(2)}, u32[]{:S(2)}) %all-to-all-start.1) | async-done | bytes 786464 | tf_op jit(solution)/shard_map/all_to_all | solution.py:57
  47.1 29.6 %all_to_all.8 = bf16[32,64,192]{2,1,0:T(8,128)(2,1)S(1)} all-to-all(bf16[32,64,192]{2,1,0:T(8,128)(2,1)S(1)} %copy.28), channel_id=1, replica_groups=mesh['ia'=4,'ja'=4,'aux'=2] {'ia','ja','aux'}, dimensions={0} | all-to-all | bytes 1572864 | tf_op jit(solution)/shard_map/all_to_all | solution.py:56
  76.7 7.3 %fusion.11 = bf16[2048,384]{0,1:T(8,128)(2,1)S(1)} fusion(bf16[2048,2048]{1,0:T(8,128)(2,1)} %param.5, bf16[2048,192]{1,0:T(8,128)(2,1)} %bitcast.5, bf16[2048,192]{1,0:T(8,128)(2,1)S(1)} %bitcast.88), kind=kOutput, calls=%fused_computation.15 | convolution fusion | flops 3225157632 | bytes 11534336 | tf_op jit(solution)/shard_map/dot_general | solution.py:32
  84.1 1.1 fusion.18
  85.2 0.0 all-gather.2.cloned.1.call-update
  85.2 0.0 reduce-scatter.2.cloned.1.call-start
  85.2 1.6 collective-permute-start
  86.8 26.5 %collective-permute-done = bf16[1,2048,3,64]{1,3,0,2:T(8,128)(2,1)S(1)} collective-permute-done((bf16[1,2048,3,64]{1,3,0,2:T(8,128)(2,1)S(1)}, bf16[1,2048,3,64]{1,3,0,2:T(8,128)(2,1)S(1)}, u32[]{:S(2)}, u32[]{:S(2)}) %collective-permute-start) | collective-permute-done | bytes 786464 | tf_op jit(solution)/shard_map/ppermute | solution.py:20
  113.3 0.1 broadcast_select_fusion.5
  113.4 0.0 copy-start
  113.4 0.0 copy-start.1
  113.4 0.9 copy-done
  114.3 0.1 pad_maximum_fusion.2
  114.5 0.0 copy-done.1
  114.5 0.0 collective-permute-start.1
  114.6 3.5 %collective-permute-done.1 = bf16[2,2048,3,64]{1,3,0,2:T(8,128)(2,1)} collective-permute-done((bf16[2,2048,3,64]{1,3,0,2:T(8,128)(2,1)S(1)}, bf16[2,2048,3,64]{1,3,0,2:T(8,128)(2,1)}, u32[]{:S(2)}, u32[]{:S(2)}) %collective-permute-start.1) | collective-permute-done | bytes 1572896 | tf_op jit(solution)/shard_map/ppermute | solution.py:20
  118.1 2.1 broadcast_select_fusion.3
  120.2 0.0 copy-start.4
  120.2 0.0 copy-start.5
  120.2 2.0 pad_maximum_fusion.1
  122.2 1.7 collective-permute-start.2
  123.9 0.0 copy-done.4
  123.9 0.1 dynamic_slice.17
  124.0 0.0 copy-done.5
  124.0 0.1 fusion.19
  124.1 0.1 broadcast_add_fusion
  124.2 1.4 broadcast_subtract_fusion
  125.6 67.0 %collective-permute-done.2 = bf16[4,2048,3,64]{1,3,0,2:T(8,128)(2,1)} collective-permute-done((bf16[4,2048,3,64]{1,3,0,2:T(8,128)(2,1)}, bf16[4,2048,3,64]{1,3,0,2:T(8,128)(2,1)}, u32[]{:S(2)}, u32[]{:S(2)}) %collective-permute-start.2) | collective-permute-done | bytes 3145760 | tf_op jit(solution)/shard_map/ppermute | solution.py:20
  192.7 2.1 broadcast_select_fusion.1
  194.8 3.2 %pad_maximum_fusion = bf16[8,2048,3,64]{1,3,0,2:T(8,128)(2,1)} fusion(bf16[4,2048,3,64]{1,3,0,2:T(8,128)(2,1)S(1)} %get-tuple-element.6, bf16[4,2048,3,64]{1,3,0,2:T(8,128)(2,1)S(1)} %get-tuple-element.5), kind=kLoop, calls=%fused_computation | loop fusion | flops 3145728 | bytes 12582912 | tf_op jit(solution)/shard_map/concatenate | solution.py:22
  197.9 8.4 %fusion = f32[3,256,3,512]{3,1,2,0:T(8,128)S(1)} fusion(bf16[2048,3,512]{0,2,1:T(8,128)(2,1)} %all-gather.2.cloned.1.call-done, bf16[2048,3,512]{0,2,1:T(8,128)(2,1)} %bitcast.79, s32[]{:T(128)S(6)} %select_n.56), kind=kOutput, calls=%fused_computation.1 | convolution fusion | flops 4831838208 | bytes 14155780 | tf_op jit(solution)/shard_map/dot_general | solution.py:70
  206.3 0.0 copy-done.2
  206.4 5.9 %fusion.3 = bf16[3,256,3,512]{3,1,2,0:T(8,128)(2,1)S(1)} fusion(f32[3,256,3,512]{3,1,2,0:T(8,128)S(1)} %fusion, bf16[3,512,2048,1]{2,1,3,0:T(8,128)(2,1)S(1)} %bitcast.80, bf16[2048,3,512]{0,2,1:T(8,128)(2,1)S(1)} %copy-done.6, s32[]{:T(128)S(6)} %select_n.56, f32[3]{0:T(128)S(1)} %get-tuple-element.14, f32[3,256,512]{2,1,0:T(8,128)S(1)} %copy-done.3), kind=kOutput, calls=%fused_computation.5 | convolution fusion | flops 4837736448 | bytes 18088452 | tf_op jit(solution)/shard_map/dot_general | solution.py:76
  212.3 2.0 copy.35
  214.3 0.8 copy.41
  215.1 7.1 %fusion.20 = f32[2048,768]{1,0:T(8,128)} fusion(bf16[2048,1536]{0,1:T(8,128)(2,1)S(1)} %bitcast.89, bf16[768,1536]{1,0:T(8,128)(2,1)S(1)} %bitcast.87), kind=kOutput, calls=%fused_computation.31 | convolution fusion | flops 4831838208 | bytes 14942208 | tf_op jit(solution)/shard_map/dot_general | solution.py:99
  222.2 0.0 reduce-scatter.2.cloned.1.call-update
  222.2 58.0 %reduce-scatter.2.cloned.1.call-done = f32[512,768]{1,0:T(8,128)} async-done(((f32[2048,768]{1,0:T(8,128)}), f32[512,768]{1,0:T(8,128)}) %reduce-scatter.2.cloned.1.call-update) | async-done | bytes 1572880 | tf_op jit(solution)/shard_map/reduce_scatter | solution.py:98
  280.2 1.9 copy.36
  282.0 1.6 copy.37
  (6 shorter events, 0.0 us)
Async XLA Ops:
  13.5 33.6 %all-to-all-start.1 = ((bf16[32,64,192]{2,1,0:T(8,128)(2,1)}), bf16[32,64,192]{2,1,0:T(8,128)(2,1)}, u32[]{:S(2)}, u32[]{:S(2)}) async-start(bf16[32,64,192]{2,1,0:T(8,128)(2,1)} %copy.30), calls=%async_computation.1 | async-start | bytes 2097152 | tf_op jit(solution)/shard_map/all_to_all | solution.py:57
  20.9 177.0 %all-gather.2.cloned.1.call-start = ((), (), s32[]{:S(2)}) async-start(), calls=%async_computation.3 | async-start | bytes 7077888 | tf_op jit(solution)/shard_map/all_gather | solution.py:64
  85.2 195.0 %reduce-scatter.2.cloned.1.call-start = ((), (), s32[]{:S(2)}) async-start(), calls=%async_computation.4 | async-start | bytes 7864320 | tf_op jit(solution)/shard_map/reduce_scatter | solution.py:98
  85.2 28.1 %collective-permute-start = (bf16[1,2048,3,64]{1,3,0,2:T(8,128)(2,1)S(1)}, bf16[1,2048,3,64]{1,3,0,2:T(8,128)(2,1)S(1)}, u32[]{:S(2)}, u32[]{:S(2)}) collective-permute-start(bf16[1,2048,3,64]{1,3,0,2:T(8,128)(2,1)S(1)} %bitcast.85), channel_id=1, source_target_pairs={{0,1},{1,0},{2,3},{3,2},{4,5},{5,4},{6,7},{7,6},{8,9},{9,8},{10,11... | collective-permute-start | bytes 2359304 | tf_op jit(solution)/shard_map/ppermute | solution.py:20
  113.4 1.0 copy-start
  113.4 1.1 copy-start.1
  114.5 3.6 %collective-permute-start.1 = (bf16[2,2048,3,64]{1,3,0,2:T(8,128)(2,1)S(1)}, bf16[2,2048,3,64]{1,3,0,2:T(8,128)(2,1)}, u32[]{:S(2)}, u32[]{:S(2)}) collective-permute-start(bf16[2,2048,3,64]{1,3,0,2:T(8,128)(2,1)S(1)} %pad_maximum_fusion.2), channel_id=1, source_target_pairs={{0,2},{1,3},{2,0},{3,1},{4,6},{5,7},{6,4},{7,5},{8,10},{9,11},{10,... | collective-permute-start | bytes 4718600 | tf_op jit(solution)/shard_map/ppermute | solution.py:20
  120.2 3.8 %copy-start.4 = (f32[512]{0:T(512)S(1)}, f32[512]{0:T(512)}, u32[]{:S(2)}) copy-start(f32[512]{0:T(512)} %param.7) | copy-start | bytes 6148
  120.2 3.8 %copy-start.5 = (f32[12]{0:T(128)S(1)}, f32[12]{0:T(128)}, u32[]{:S(2)}) copy-start(f32[12]{0:T(128)} %param.6) | copy-start | bytes 148
  122.2 70.5 %collective-permute-start.2 = (bf16[4,2048,3,64]{1,3,0,2:T(8,128)(2,1)}, bf16[4,2048,3,64]{1,3,0,2:T(8,128)(2,1)}, u32[]{:S(2)}, u32[]{:S(2)}) collective-permute-start(bf16[4,2048,3,64]{1,3,0,2:T(8,128)(2,1)} %pad_maximum_fusion.1), channel_id=1, source_target_pairs={{0,4},{1,5},{2,6},{3,7},{4,0},{5,1},{6,2},{7,3},{8,12},{9,13},{10,... | collective-permute-start | bytes 9437192 | tf_op jit(solution)/shard_map/ppermute | solution.py:20
  197.9 8.4 %copy-start.2 = (bf16[8,2048,3,64]{1,3,0,2:T(8,128)(2,1)S(1)}, bf16[8,2048,3,64]{1,3,0,2:T(8,128)(2,1)}, u32[]{:S(2)}) copy-start(bf16[8,2048,3,64]{1,3,0,2:T(8,128)(2,1)} %pad_maximum_fusion) | copy-start | bytes 18874372
  197.9 8.4 %copy-start.3 = (f32[3,256,512]{2,1,0:T(8,128)S(1)}, f32[3,256,512]{2,1,0:T(8,128)}, u32[]{:S(2)}) copy-start(f32[3,256,512]{2,1,0:T(8,128)} %broadcast_subtract_fusion) | copy-start | bytes 4718596
  197.9 8.4 %copy-start.6 = (bf16[2048,3,512]{0,2,1:T(8,128)(2,1)S(1)}, bf16[2048,3,512]{0,2,1:T(8,128)(2,1)}, u32[]{:S(2)}) copy-start(bf16[2048,3,512]{0,2,1:T(8,128)(2,1)} %all-gather.2.cloned.1.call-done) | copy-start | bytes 18874372
Sparse Core Ops, SparseCore 0:
  85.3 101.0 all-gather.1
  222.3 57.7 reduce-scatter.1
